TPU v7x, 32 devices: a whole 2x2x4 slice. The times are simulated.
32 devices in a mesh: dp: 8 (over z, core), tensor: 4 (over y, x).
Axes of the slice: x: 2, y: 2, z: 4, core: 2. Of those that a mesh axis runs over, the one named last changes fastest.
Arguments:
- tokens: bfloat16 [8192, 2048], P(('dp', 'tensor')), may hold values from -6 to 6
- w_qkv: bfloat16 [2048, 6144], P('dp', 'tensor'), may hold values from -0.125 to 0.125
- w_out: bfloat16 [2048, 2048], P('tensor', 'dp'), may hold values from -1 to 1
- w_up: bfloat16 [2048, 8192], P('dp', 'tensor'), may hold values from -0.125 to 0.125
- w_down: bfloat16 [8192, 2048], P('tensor', 'dp'), may hold values from -0.0625 to 0.0625
- w_ada: float32 [256, 8192], P(None, ('dp', 'tensor')), may hold values from -0.1875 to 0.1875
- b_ada: float32 [8192], P(('dp', 'tensor')), may hold values from -1.8 to 1.8
- timesteps: int32 [32], replicated, may hold values from 0 to 999
- image_len: int32 [32], replicated, may hold values from 64 to 1024, as said below
- cotangent: bfloat16 [8192, 2048], P(('dp', 'tensor')), may hold values from -6 to 6
Outputs:
- output: bfloat16 [8192, 2048], P(('dp', 'tensor'))
- grad_input: float32 [8192, 2048], P(('dp', 'tensor'))
- grad_w_qkv: float32 [2048, 6144], P('dp', 'tensor')
- grad_w_out: float32 [2048, 2048], P('tensor', 'dp')
- grad_w_up: float32 [2048, 8192], P('dp', 'tensor')
- grad_w_down: float32 [8192, 2048], P('tensor', 'dp')
- grad_w_ada: float32 [256, 8192], P(None, ('dp', 'tensor'))
- grad_b_ada: float32 [8192], P(('dp', 'tensor'))
Inputs may be any that keep to these rules, and one draw needn't show every extreme that they name: `image_len`: 4 images have 1024 tokens, 12 have 1024 // 4 and the rest 1024 // 16; the lengths sum to 8192.
All inputs are finite; a program needn't handle non-finite values.
Results may differ from a plain program's by a relative error of at most 0.012.
Values may be sent and summed in bfloat16 or wider, within the bound.
No kernel may reach another device: no remote copies, remote signals or barrier semaphores. Data moves between devices by JAX's collectives and lax.ppermute only.
A program may use at most 256 MiB of HBM per device.

v0:
```python
import math

import jax
import jax.numpy as jnp
from jax import lax
from jax.sharding import PartitionSpec as P

HD = 128
LONG = 1024


epsilon = 1e-06
highest = lax.Precision.HIGHEST


def extended_2(block, sides, width):
    for axis, dim in sides:
        count = lax.axis_size(axis)
        forward = [(i, i + 1) for i in range(count - 1)]
        forward.append((count - 1, 0))
        backward = [(target, source) for source, target in forward]
        low = lax.ppermute(
            lax.slice_in_dim(block, block.shape[dim] - width, None, axis=dim), axis, forward
        )
        high = lax.ppermute(lax.slice_in_dim(block, 0, width, axis=dim), axis, backward)
        block = jnp.concatenate([low, block, high], axis=dim)
    return block


def frequency_table(timesteps, columns):
    half_cols = columns // 2
    rates = jnp.exp(-math.log(10000.0) * jnp.arange(half_cols, dtype=jnp.float32) / half_cols)
    angles = timesteps.astype(jnp.float32)[:, None] * rates[None, :]
    return jnp.concatenate([jnp.cos(angles), jnp.sin(angles)], axis=1)


def segment_of(positions, image_len):
    starts = jnp.cumsum(image_len, dtype=jnp.int32) - image_len
    inside = (starts[None, :] <= positions[:, None]).astype(jnp.int32)
    return jnp.sum(inside, axis=1, dtype=jnp.int32) - 1


def norm_mod(rows_in, scale_cols, shift_cols):
    factor = lax.rsqrt(jnp.mean(rows_in * rows_in, axis=-1, keepdims=True) + epsilon)
    return rows_in * factor * (1.0 + scale_cols) + shift_cols


def gelu_tanh(values):
    return jax.nn.gelu(values, approximate=True)


def fetch_weights(qkv_part, out_part, up_part, down_part):
    return (
        lax.all_gather(qkv_part, "dp", axis=0, tiled=True),
        lax.all_gather(out_part, "dp", axis=1, tiled=True),
        lax.all_gather(up_part, "dp", axis=0, tiled=True),
        lax.all_gather(down_part, "dp", axis=1, tiled=True),
    )


def spread_rows(values):
    return lax.all_gather(values, "tensor", axis=0, tiled=True)


def fold_rows(values):
    return lax.psum_scatter(values, "tensor", scatter_dimension=0, tiled=True)


def local(tokens, w_qkv, w_out, w_up, w_down, w_ada, b_ada, timesteps, image_len, cotangent):
    n_tensor = lax.axis_size("tensor")
    n_data = lax.axis_size("dp")
    rows_dev = tokens.shape[0]
    tok_dev = rows_dev * n_tensor
    total_tok = tok_dev * n_data
    shift_pos = LONG // 32
    q_rows = min(512, LONG)
    window = q_rows + 2 * tok_dev
    n_blocks = tok_dev // q_rows
    heads_local = w_qkv.shape[1] // (3 * HD)
    head_cols = heads_local * HD
    score_scale = HD ** (-0.5)
    n_images = image_len.shape[0]
    data_idx = lax.axis_index("dp")
    tensor_idx = lax.axis_index("tensor")
    row_start = (data_idx * n_tensor + tensor_idx) * rows_dev
    row_pos = jnp.mod(row_start + jnp.arange(rows_dev, dtype=jnp.int32) + shift_pos, total_tok)
    seg_rows = segment_of(row_pos, image_len)
    ext_start = data_idx * tok_dev - tok_dev + total_tok
    ext_pos = jnp.mod(ext_start + jnp.arange(3 * tok_dev, dtype=jnp.int32) + shift_pos, total_tok)
    seg_ext = segment_of(ext_pos, image_len)
    full_qkv, full_out, full_up, full_down = fetch_weights(w_qkv, w_out, w_up, w_down)
    freq = frequency_table(timesteps, w_ada.shape[0])
    mod_cols = jnp.dot(freq, w_ada, precision=highest) + b_ada[None, :]
    modulation = lax.all_gather(mod_cols, ("dp", "tensor"), axis=1, tiled=True)
    image_ids = jnp.arange(n_images, dtype=jnp.int32)[None, :]
    onehot_rows = (seg_rows[:, None] == image_ids).astype(jnp.float32)
    mod_rows = jnp.dot(onehot_rows, modulation, precision=highest)
    width = modulation.shape[1] // 4
    scale_one = mod_rows[:, 0:width]
    shift_one = mod_rows[:, width : 2 * width]
    scale_two = mod_rows[:, 2 * width : 3 * width]
    shift_two = mod_rows[:, 3 * width : 4 * width]
    inputs_f = tokens.astype(jnp.float32)
    normed_one = norm_mod(inputs_f, scale_one, shift_one).astype(jnp.bfloat16)
    normed_full = spread_rows(normed_one)
    qkv = jnp.dot(normed_full, full_qkv, preferred_element_type=jnp.float32).astype(jnp.bfloat16)
    qkv = qkv.reshape(tok_dev, heads_local, 3, HD)
    queries = qkv[:, :, 0]
    key_rows = qkv[:, :, 1]
    value_rows = qkv[:, :, 2]
    pair_rows = jnp.concatenate(
        [key_rows.reshape(tok_dev, head_cols), value_rows.reshape(tok_dev, head_cols)], axis=1
    )
    extended = extended_2(pair_rows, (("dp", 0),), tok_dev)
    key_ext = extended[:, :head_cols].reshape(3 * tok_dev, heads_local, HD)
    value_ext = extended[:, head_cols:].reshape(3 * tok_dev, heads_local, HD)

    def block_scores(start_row):
        q_block = queries[start_row : start_row + q_rows]
        k_window = key_ext[start_row : start_row + window]
        raw = (
            jnp.einsum("qhd,khd->hqk", q_block, k_window, preferred_element_type=jnp.float32)
            * score_scale
        )
        seg_query = seg_ext[tok_dev + start_row : tok_dev + start_row + q_rows]
        seg_key = seg_ext[start_row : start_row + window]
        same = seg_query[:, None] == seg_key[None, :]
        return jnp.where(same[None], raw, -1e30)

    out_blocks = []
    log_sums = []
    for block_id in range(n_blocks):
        start_row = block_id * q_rows
        scores = block_scores(start_row)
        row_max = jnp.max(scores, axis=-1, keepdims=True)
        shifted = jnp.exp(scores - row_max)
        row_total = jnp.sum(shifted, axis=-1, keepdims=True)
        weights_lo = (shifted / row_total).astype(jnp.bfloat16)
        log_sums.append(row_max + jnp.log(row_total))
        out_blocks.append(
            jnp.einsum(
                "hqk,khd->qhd",
                weights_lo,
                value_ext[start_row : start_row + window],
                preferred_element_type=jnp.float32,
            )
        )
    attn_f = jnp.concatenate(out_blocks, axis=0)
    attn_lo = attn_f.astype(jnp.bfloat16).reshape(tok_dev, head_cols)
    attn_part = jnp.dot(attn_lo, full_out, preferred_element_type=jnp.float32)
    branch = fold_rows(attn_part)
    mid_rows = inputs_f + branch
    normed_two = norm_mod(mid_rows, scale_two, shift_two).astype(jnp.bfloat16)
    normed_two_full = spread_rows(normed_two)
    up_rows = jnp.dot(normed_two_full, full_up, preferred_element_type=jnp.float32)
    act_rows = gelu_tanh(up_rows).astype(jnp.bfloat16)
    mlp_part = jnp.dot(act_rows, full_down, preferred_element_type=jnp.float32)
    mlp_out = fold_rows(mlp_part)
    result = (mid_rows + mlp_out).astype(jnp.bfloat16)
    held = lax.optimization_barrier((w_qkv, w_out, w_up, w_down, cotangent))
    full_qkv, full_out, full_up, full_down = fetch_weights(held[0], held[1], held[2], held[3])
    grad_rows = cotangent.astype(jnp.float32)
    grad_full = spread_rows(cotangent)
    grad_downw = jnp.einsum("tf,td->fd", act_rows, grad_full, preferred_element_type=jnp.float32)
    d_act = jnp.einsum("td,fd->tf", grad_full, full_down, preferred_element_type=jnp.float32)
    gelu_pull = jax.vjp(gelu_tanh, up_rows)[1]
    d_up = gelu_pull(d_act)[0].astype(jnp.bfloat16)
    grad_upw = jnp.einsum("td,tf->df", normed_two_full, d_up, preferred_element_type=jnp.float32)
    d_h2_part = jnp.einsum("tf,df->td", d_up, full_up, preferred_element_type=jnp.float32)
    d_h2 = fold_rows(d_h2_part)
    norm_two_pull = jax.vjp(norm_mod, mid_rows, scale_two, shift_two)[1]
    d_mid, d_scale_two, d_shift_two = norm_two_pull(d_h2)
    d_mid = grad_rows + d_mid
    branch_full = spread_rows(d_mid.astype(jnp.bfloat16))
    grad_outw = jnp.einsum("tc,td->cd", attn_lo, branch_full, preferred_element_type=jnp.float32)
    d_attn = jnp.einsum("td,cd->tc", branch_full, full_out, preferred_element_type=jnp.float32)
    d_attn = d_attn.astype(jnp.bfloat16).reshape(tok_dev, heads_local, HD)
    d_query_blocks = []
    d_key_ext = jnp.zeros((3 * tok_dev, heads_local, HD), jnp.float32)
    d_value_ext = jnp.zeros((3 * tok_dev, heads_local, HD), jnp.float32)
    for block_id in range(n_blocks):
        start_row = block_id * q_rows
        scores = block_scores(start_row)
        softmax_f = jnp.exp(scores - log_sums[block_id])
        d_out_block = d_attn[start_row : start_row + q_rows]
        q_block = queries[start_row : start_row + q_rows]
        k_window = key_ext[start_row : start_row + window]
        v_window = value_ext[start_row : start_row + window]
        d_soft = jnp.einsum(
            "qhd,khd->hqk", d_out_block, v_window, preferred_element_type=jnp.float32
        )
        inner = jnp.sum(softmax_f * d_soft, axis=-1, keepdims=True)
        d_scores = (softmax_f * (d_soft - inner)).astype(jnp.bfloat16)
        d_query_blocks.append(
            jnp.einsum("hqk,khd->qhd", d_scores, k_window, preferred_element_type=jnp.float32)
            * score_scale
        )
        d_key_ext = d_key_ext.at[start_row : start_row + window].add(
            jnp.einsum("hqk,qhd->khd", d_scores, q_block, preferred_element_type=jnp.float32)
            * score_scale
        )
        d_value_ext = d_value_ext.at[start_row : start_row + window].add(
            jnp.einsum(
                "hqk,qhd->khd",
                softmax_f.astype(jnp.bfloat16),
                d_out_block,
                preferred_element_type=jnp.float32,
            )
        )
    stacked = jnp.concatenate(
        [d_key_ext.reshape(3 * tok_dev, head_cols), d_value_ext.reshape(3 * tok_dev, head_cols)],
        axis=1,
    )
    outer_rows = jnp.concatenate([stacked[:tok_dev], stacked[2 * tok_dev :]], axis=0)
    returned = extended_2(outer_rows.astype(jnp.bfloat16), (("dp", 0),), tok_dev).astype(
        outer_rows.dtype
    )
    own_grads = stacked[tok_dev : 2 * tok_dev] + returned[:tok_dev] + returned[3 * tok_dev :]
    d_query = jnp.concatenate(d_query_blocks, axis=0)
    d_key = own_grads[:, :head_cols].reshape(tok_dev, heads_local, HD)
    d_value = own_grads[:, head_cols:].reshape(tok_dev, heads_local, HD)
    d_qkv = (
        jnp.stack([d_query, d_key, d_value], axis=2)
        .astype(jnp.bfloat16)
        .reshape(tok_dev, 3 * head_cols)
    )
    grad_qkvw = jnp.einsum("td,tc->dc", normed_full, d_qkv, preferred_element_type=jnp.float32)
    d_h1_part = jnp.einsum("tc,dc->td", d_qkv, full_qkv, preferred_element_type=jnp.float32)
    d_h1 = fold_rows(d_h1_part)
    norm_one_pull = jax.vjp(norm_mod, inputs_f, scale_one, shift_one)[1]
    d_inputs, d_scale_one, d_shift_one = norm_one_pull(d_h1)
    grad_input = d_mid + d_inputs
    d_mod_rows = jnp.concatenate([d_scale_one, d_shift_one, d_scale_two, d_shift_two], axis=1)
    d_mod = jnp.dot(onehot_rows.T, d_mod_rows, precision=highest)
    d_mod_cols = lax.psum_scatter(d_mod, ("dp", "tensor"), scatter_dimension=1, tiled=True)
    grad_adaw = jnp.dot(freq.T, d_mod_cols, precision=highest)
    grad_bias = jnp.sum(d_mod_cols, axis=0)
    grad_qkvw, grad_outw, grad_upw, grad_downw = (
        lax.psum_scatter(grad_qkvw, "dp", scatter_dimension=0, tiled=True),
        lax.psum_scatter(grad_outw, "dp", scatter_dimension=1, tiled=True),
        lax.psum_scatter(grad_upw, "dp", scatter_dimension=0, tiled=True),
        lax.psum_scatter(grad_downw, "dp", scatter_dimension=1, tiled=True),
    )
    return (result, grad_input, grad_qkvw, grad_outw, grad_upw, grad_downw, grad_adaw, grad_bias)


def solution(mesh):
    in_specs = (
        P(("dp", "tensor"), None),
        P("dp", "tensor"),
        P("tensor", "dp"),
        P("dp", "tensor"),
        P("tensor", "dp"),
        P(None, ("dp", "tensor")),
        P(("dp", "tensor")),
        P(),
        P(),
        P(("dp", "tensor"), None),
    )
    out_specs = (
        P(("dp", "tensor"), None),
        P(("dp", "tensor"), None),
        P("dp", "tensor"),
        P("tensor", "dp"),
        P("dp", "tensor"),
        P("tensor", "dp"),
        P(None, ("dp", "tensor")),
        P(("dp", "tensor")),
    )
    return jax.shard_map(local, mesh=mesh, in_specs=in_specs, out_specs=out_specs, check_vma=False)
```

profile of v0, /device:TPU:0, one launch (start us, length us, event | category | flops | bytes accessed | tf_op | source)
XLA Modules:
  0.0 2089.3 jit_solution(2173259746253641887)
XLA Ops:
  14.2 51.5 %all-gather.14.cloned.1.call-done = f32[32,8192]{1,0:T(8,128)} async-done(((f32[32,256]{1,0:T(8,128)}), f32[32,8192]{1,0:T(8,128)}) %all-gather.14.cloned.1.call-update) | async-done | bytes 1048592 | tf_op jit(solution)/shard_map/all_gather | solution.py:94
  76.1 51.6 %all-gather.16.cloned.1.call-done = bf16[1024,2048]{1,0:T(8,128)(2,1)} async-done(((bf16[256,2048]{1,0:T(8,128)(2,1)}), bf16[1024,2048]{1,0:T(8,128)(2,1)}) %all-gather.16.cloned.1.call-update) | async-done | bytes 4194320 | tf_op jit(solution)/shard_map/all_gather | solution.py:62
  127.8 66.4 %all-gather.18.cloned.1.call-done = bf16[2048,1536]{1,0:T(8,128)(2,1)} async-done(((bf16[256,1536]{1,0:T(8,128)(2,1)}), bf16[2048,1536]{1,0:T(8,128)(2,1)}) %all-gather.18.cloned.1.call-update) | async-done | bytes 6291472 | tf_op jit(solution)/shard_map/all_gather | solution.py:54
  194.1 11.2 convolution_convert_fusion
  217.0 59.4 %collective-permute-done.1 = bf16[1024,1024]{0,1:T(8,128)(2,1)} collective-permute-done((bf16[1024,1024]{0,1:T(8,128)(2,1)}, bf16[1024,1024]{0,1:T(8,128)(2,1)}, u32[]{:S(2)}, u32[]{:S(2)}) %collective-permute-start.1) | collective-permute-done | bytes 2097184 | tf_op jit(solution)/shard_map/ppermute | solution.py:25
  279.4 17.6 pad_maximum_fusion.1
  301.0 6.4 fusion.85
  314.9 11.0 fusion.55
  326.0 6.4 fusion.86
  339.4 9.8 fusion.56
  349.3 7.4 fusion.60
  357.3 84.6 %reduce-scatter.10.cloned.1.call-done = f32[256,2048]{1,0:T(8,128)} async-done(((f32[1024,2048]{1,0:T(8,128)}), f32[256,2048]{1,0:T(8,128)}) %reduce-scatter.10.cloned.1.call-update) | async-done | bytes 2097168 | tf_op jit(solution)/shard_map/reduce_scatter | solution.py:66
  450.4 75.1 %all-gather.24.cloned.1.call-done = bf16[2048,2048]{1,0:T(8,128)(2,1)} async-done(((bf16[256,2048]{1,0:T(8,128)(2,1)}), bf16[2048,2048]{1,0:T(8,128)(2,1)}) %all-gather.24.cloned.1.call-update) | async-done | bytes 8388624 | tf_op jit(solution)/shard_map/all_gather | solution.py:56
  525.5 53.5 %all-gather.22.cloned.1.call-done = bf16[1024,2048]{1,0:T(8,128)(2,1)} async-done(((bf16[256,2048]{1,0:T(8,128)(2,1)}), bf16[1024,2048]{1,0:T(8,128)(2,1)}) %all-gather.22.cloned.1.call-update) | async-done | bytes 4194320 | tf_op jit(solution)/shard_map/all_gather | solution.py:62
  579.0 14.6 fusion.87
  593.6 39.8 %all-gather.30.cloned.1.call-done = bf16[1024,2048]{1,0:T(8,128)(2,1)} async-done(((bf16[256,2048]{1,0:T(8,128)(2,1)}), bf16[1024,2048]{1,0:T(8,128)(2,1)}) %all-gather.30.cloned.1.call-update) | async-done | bytes 4194320 | tf_op jit(solution)/shard_map/all_gather | solution.py:62
  633.5 84.1 %all-gather.28.cloned.1.call-done = bf16[2048,2048]{1,0:T(8,128)(2,1)} async-done(((bf16[2048,256]{1,0:T(8,128)(2,1)}), bf16[2048,2048]{1,0:T(8,128)(2,1)}) %all-gather.28.cloned.1.call-update) | async-done | bytes 8388624 | tf_op jit(solution)/shard_map/all_gather | solution.py:57
  717.6 19.8 fusion.19
  737.4 61.9 %all-gather.32.cloned.1.call-done = bf16[2048,2048]{1,0:T(8,128)(2,1)} async-done(((bf16[256,2048]{1,0:T(8,128)(2,1)}), bf16[2048,2048]{1,0:T(8,128)(2,1)}) %all-gather.32.cloned.1.call-update) | async-done | bytes 8388624 | tf_op jit(solution)/shard_map/all_gather | solution.py:56
  799.3 14.7 fusion.88
  814.1 67.8 %all-gather.26.cloned.1.call-done = bf16[2048,2048]{1,0:T(8,128)(2,1)} async-done(((bf16[2048,256]{1,0:T(8,128)(2,1)}), bf16[2048,2048]{1,0:T(8,128)(2,1)}) %all-gather.26.cloned.1.call-update) | async-done | bytes 8388624 | tf_op jit(solution)/shard_map/all_gather | solution.py:57
  881.9 16.3 fusion.75
  898.9 70.4 %reduce-scatter.14.cloned.1.call-done = f32[256,2048]{1,0:T(8,128)} async-done(((f32[1024,2048]{1,0:T(8,128)}), f32[256,2048]{1,0:T(8,128)}) %reduce-scatter.14.cloned.1.call-update) | async-done | bytes 2097168 | tf_op jit(solution)/shard_map/reduce_scatter | solution.py:66
  971.9 86.8 %reduce-scatter.12.cloned.1.call-done = f32[256,2048]{1,0:T(8,128)} async-done(((f32[1024,2048]{1,0:T(8,128)}), f32[256,2048]{1,0:T(8,128)}) %reduce-scatter.12.cloned.1.call-update) | async-done | bytes 2097168 | tf_op jit(solution)/shard_map/reduce_scatter | solution.py:66
  1058.7 6.5 fusion.76
  1065.9 24.9 %all-gather.36.cloned.1.call-done = bf16[512,2048]{1,0:T(8,128)(2,1)} async-done(((bf16[512,256]{1,0:T(8,128)(2,1)}), bf16[512,2048]{1,0:T(8,128)(2,1)}) %all-gather.36.cloned.1.call-update) | async-done | bytes 2097168 | tf_op jit(solution)/shard_map/all_gather | solution.py:55
  1090.8 53.9 %all-gather.34.cloned.1.call-done = bf16[1024,2048]{1,0:T(8,128)(2,1)} async-done(((bf16[256,2048]{1,0:T(8,128)(2,1)}), bf16[1024,2048]{1,0:T(8,128)(2,1)}) %all-gather.34.cloned.1.call-update) | async-done | bytes 4194320 | tf_op jit(solution)/shard_map/all_gather | solution.py:62
  1150.0 10.7 fusion.33
  1160.7 13.5 multiply_reduce_fusion.1
  1177.8 14.7 multiply_convert_fusion.1
  1198.2 13.3 multiply_reduce_fusion
  1211.5 14.5 multiply_convert_fusion
  1233.6 15.2 fusion.31
  1248.9 8.2 fusion.4
  1265.5 8.4 fusion.57
  1273.9 6.1 fusion.58
  1281.2 29.0 %collective-permute-done.2 = bf16[1024,1024]{0,1:T(8,128)(2,1)} collective-permute-done((bf16[1024,1024]{0,1:T(8,128)(2,1)}, bf16[1024,1024]{0,1:T(8,128)(2,1)}, u32[]{:S(2)}, u32[]{:S(2)}) %collective-permute-start.2) | collective-permute-done | bytes 2097184 | tf_op jit(solution)/shard_map/ppermute | solution.py:22
  1318.3 10.8 fusion.89
  1329.2 86.0 %reduce-scatter.16.cloned.1.call-done = f32[256,2048]{1,0:T(8,128)} async-done(((f32[1024,2048]{1,0:T(8,128)}), f32[256,2048]{1,0:T(8,128)}) %reduce-scatter.16.cloned.1.call-update) | async-done | bytes 2097168 | tf_op jit(solution)/shard_map/reduce_scatter | solution.py:66
  1426.8 6.5 fusion.59
  1433.4 16.8 fusion.74
  1450.2 15.2 fusion.91
  1467.3 11.5 fusion.90
  1478.9 84.4 %reduce-scatter.26.cloned.1.call-done = f32[32,256]{1,0:T(8,128)} async-done(((f32[32,8192]{1,0:T(8,128)}), f32[32,256]{1,0:T(8,128)}) %reduce-scatter.26.cloned.1.call-update) | async-done | bytes 32784 | tf_op jit(solution)/shard_map/reduce_scatter | solution.py:235
  1566.6 45.8 %reduce-scatter.20.cloned.1.call-done = f32[512,256]{1,0:T(8,128)} async-done(((f32[512,2048]{1,0:T(8,128)}), f32[512,256]{1,0:T(8,128)}) %reduce-scatter.20.cloned.1.call-update) | async-done | bytes 524304 | tf_op jit(solution)/shard_map/reduce_scatter | solution.py:240
  1612.4 169.5 %reduce-scatter.24.cloned.1.call-done = f32[2048,256]{1,0:T(8,128)} async-done(((f32[2048,2048]{1,0:T(8,128)}), f32[2048,256]{1,0:T(8,128)}) %reduce-scatter.24.cloned.1.call-update) | async-done | bytes 2097168 | tf_op jit(solution)/shard_map/reduce_scatter | solution.py:242
  1781.9 169.6 %reduce-scatter.22.cloned.1.call-done = f32[256,2048]{1,0:T(8,128)} async-done(((f32[2048,2048]{1,0:T(8,128)}), f32[256,2048]{1,0:T(8,128)}) %reduce-scatter.22.cloned.1.call-update) | async-done | bytes 2097168 | tf_op jit(solution)/shard_map/reduce_scatter | solution.py:241
  1951.4 130.5 %reduce-scatter.18.cloned.1.call-done = f32[256,1536]{1,0:T(8,128)} async-done(((f32[2048,1536]{1,0:T(8,128)}), f32[256,1536]{1,0:T(8,128)}) %reduce-scatter.18.cloned.1.call-update) | async-done | bytes 1572880 | tf_op jit(solution)/shard_map/reduce_scatter | solution.py:239
  (194 shorter events, 120.0 us)
Async XLA Ops:
  7.2 58.5 %all-gather.14.cloned.1.call-start = ((), (), s32[]{:S(2)}) async-start(), calls=%async_computation.9 | async-start | bytes 1081344 | tf_op jit(solution)/shard_map/all_gather | solution.py:94
  10.2 117.5 %all-gather.16.cloned.1.call-start = ((), (), s32[]{:S(2)}) async-start(), calls=%async_computation.10 | async-start | bytes 5242880 | tf_op jit(solution)/shard_map/all_gather | solution.py:62
  12.0 61.7 %copy-start.9 = (bf16[256,2048]{1,0:T(8,128)(2,1)S(1)}, bf16[256,2048]{1,0:T(8,128)(2,1)}, u32[]{:S(2)}) copy-start(bf16[256,2048]{1,0:T(8,128)(2,1)} %param.18) | copy-start | bytes 3145732
  14.2 61.1 %copy-start.33 = (f32[256]{0:T(256)}, f32[256]{0:T(256)S(1)}, u32[]{:S(2)}) copy-start(f32[256]{0:T(256)S(1)} %fusion.67) | copy-start | bytes 3076
  14.2 61.1 %copy-start.29 = (s32[256]{0:T(256)}, s32[256]{0:T(256)S(1)}, u32[]{:S(2)}) copy-start(s32[256]{0:T(256)S(1)} %broadcast_add_fusion.1) | copy-start | bytes 3076
  75.3 118.8 %all-gather.18.cloned.1.call-start = ((), (), s32[]{:S(2)}) async-start(), calls=%async_computation.11 | async-start | bytes 7077888 | tf_op jit(solution)/shard_map/all_gather | solution.py:54
  76.1 273.2 %all-gather.20.cloned.1.call-start = ((), (), s32[]{:S(2)}) async-start(), calls=%async_computation.12 | async-start | bytes 2359296 | tf_op jit(solution)/shard_map/all_gather | solution.py:55
  213.3 63.1 %collective-permute-start.1 = (bf16[1024,1024]{0,1:T(8,128)(2,1)}, bf16[1024,1024]{0,1:T(8,128)(2,1)}, u32[]{:S(2)}, u32[]{:S(2)}) collective-permute-start(bf16[1024,1024]{0,1:T(8,128)(2,1)} %pad_maximum_fusion.6), channel_id=1, source_target_pairs={{4,0},{8,4},{12,8},{16,12},{20,16},{24,20},{28,24},{0,28},{5,1},{9... | collective-permute-start | bytes 6291464 | tf_op jit(solution)/shard_map/ppermute | solution.py:25
  213.9 65.4 %collective-permute-start = (bf16[1024,1024]{0,1:T(8,128)(2,1)}, bf16[1024,1024]{0,1:T(8,128)(2,1)}, u32[]{:S(2)}, u32[]{:S(2)}) collective-permute-start(bf16[1024,1024]{0,1:T(8,128)(2,1)} %pad_maximum_fusion.6), channel_id=1, source_target_pairs={{0,4},{4,8},{8,12},{12,16},{16,20},{20,24},{24,28},{28,0},{1,5},{5... | collective-permute-start | bytes 6291464 | tf_op jit(solution)/shard_map/ppermute | solution.py:22
  214.0 228.0 %reduce-scatter.10.cloned.1.call-start = ((), (), s32[]{:S(2)}) async-start(), calls=%async_computation.13 | async-start | bytes 10485760 | tf_op jit(solution)/shard_map/reduce_scatter | solution.py:66
  314.4 11.5 copy-start.27
  339.4 9.9 copy-start.35
  356.7 168.8 %all-gather.24.cloned.1.call-start = ((), (), s32[]{:S(2)}) async-start(), calls=%async_computation.15 | async-start | bytes 9437184 | tf_op jit(solution)/shard_map/all_gather | solution.py:56
  357.3 221.7 %all-gather.22.cloned.1.call-start = ((), (), s32[]{:S(2)}) async-start(), calls=%async_computation.14 | async-start | bytes 5242880 | tf_op jit(solution)/shard_map/all_gather | solution.py:62
  447.5 185.9 %all-gather.30.cloned.1.call-start = ((), (), s32[]{:S(2)}) async-start(), calls=%async_computation.19 | async-start | bytes 5242880 | tf_op jit(solution)/shard_map/all_gather | solution.py:62
  448.3 269.3 %all-gather.28.cloned.1.call-start = ((), (), s32[]{:S(2)}) async-start(), calls=%async_computation.18 | async-start | bytes 9437184 | tf_op jit(solution)/shard_map/all_gather | solution.py:57
  449.0 350.3 %all-gather.32.cloned.1.call-start = ((), (), s32[]{:S(2)}) async-start(), calls=%async_computation.20 | async-start | bytes 9437184 | tf_op jit(solution)/shard_map/all_gather | solution.py:56
  449.6 432.3 %all-gather.26.cloned.1.call-start = ((), (), s32[]{:S(2)}) async-start(), calls=%async_computation.16 | async-start | bytes 9437184 | tf_op jit(solution)/shard_map/all_gather | solution.py:57
  450.3 519.0 %reduce-scatter.14.cloned.1.call-start = ((), (), s32[]{:S(2)}) async-start(), calls=%async_computation.21 | async-start | bytes 10485760 | tf_op jit(solution)/shard_map/reduce_scatter | solution.py:66
  814.0 244.7 %reduce-scatter.12.cloned.1.call-start = ((), (), s32[]{:S(2)}) async-start(), calls=%async_computation.17 | async-start | bytes 10485760 | tf_op jit(solution)/shard_map/reduce_scatter | solution.py:66
  898.2 160.5 %copy-start.16 = (bf16[256,2048]{1,0:T(8,128)(2,1)S(1)}, bf16[256,2048]{1,0:T(8,128)(2,1)}, u32[]{:S(2)}) copy-start(bf16[256,2048]{1,0:T(8,128)(2,1)} %param.27) | copy-start | bytes 3145732
  898.3 192.6 %all-gather.36.cloned.1.call-start = ((), (), s32[]{:S(2)}) async-start(), calls=%async_computation.23 | async-start | bytes 2359296 | tf_op jit(solution)/shard_map/all_gather | solution.py:55
  898.8 245.9 %all-gather.34.cloned.1.call-start = ((), (), s32[]{:S(2)}) async-start(), calls=%async_computation.22 | async-start | bytes 5242880 | tf_op jit(solution)/shard_map/all_gather | solution.py:62
  971.9 94.0 %copy-start.26 = (f32[4,512]{1,0:T(4,128)S(1)}, f32[4,512]{1,0:T(4,128)}, u32[]{:S(2)}) copy-start(f32[4,512]{1,0:T(4,128)} %copy-done.25) | copy-start | bytes 24580
  971.9 94.0 %copy-start.28 = (f32[4,512]{1,0:T(4,128)S(1)}, f32[4,512]{1,0:T(4,128)}, u32[]{:S(2)}) copy-start(f32[4,512]{1,0:T(4,128)} %copy-done.27) | copy-start | bytes 24580
  1065.2 251.4 %all-gather.38.cloned.1.call-start = ((), (), s32[]{:S(2)}) async-start(), calls=%async_computation.24 | async-start | bytes 7077888 | tf_op jit(solution)/shard_map/all_gather | solution.py:54
  1065.8 349.4 %reduce-scatter.16.cloned.1.call-start = ((), (), s32[]{:S(2)}) async-start(), calls=%async_computation.25 | async-start | bytes 10485760 | tf_op jit(solution)/shard_map/reduce_scatter | solution.py:66
  1150.0 10.7 copy-start.12
  1233.6 15.3 copy-start.6
  1261.9 48.2 %collective-permute-start.2 = (bf16[1024,1024]{0,1:T(8,128)(2,1)}, bf16[1024,1024]{0,1:T(8,128)(2,1)}, u32[]{:S(2)}, u32[]{:S(2)}) collective-permute-start(bf16[1024,1024]{0,1:T(8,128)(2,1)} %get-tuple-element.68), channel_id=1, source_target_pairs={{0,4},{4,8},{8,12},{12,16},{16,20},{20,24},{24,28},{28,0},{1,5},{5... | collective-permute-start | bytes 6291464 | tf_op jit(solution)/shard_map/ppermute | solution.py:22
  1261.9 11.9 slice-start
  1261.9 11.9 slice-start.1
  1261.9 11.9 slice-start.2
  1261.9 48.2 %collective-permute-start.3 = (bf16[1024,1024]{0,1:T(8,128)(2,1)}, bf16[1024,1024]{0,1:T(8,128)(2,1)}, u32[]{:S(2)}, u32[]{:S(2)}) collective-permute-start(bf16[1024,1024]{0,1:T(8,128)(2,1)} %get-tuple-element.69), channel_id=1, source_target_pairs={{4,0},{8,4},{12,8},{16,12},{20,16},{24,20},{28,24},{0,28},{5,1},{9... | collective-permute-start | bytes 6291464 | tf_op jit(solution)/shard_map/ppermute | solution.py:25
  1265.5 44.7 %slice-start.3 = ((s8[6291456]{0:T(1024)(128)(4,1)}), s8[4194304]{0:T(1024)(128)(4,1)S(1)}, s32[]{:S(2)}) async-start(s8[6291456]{0:T(1024)(128)(4,1)} %bitcast.110), calls=%async_computation.34 | async-start | bytes 8388608
  1273.9 36.3 %slice-start.4 = ((s8[6291456]{0:T(1024)(128)(4,1)}), s8[2097152]{0:T(1024)(128)(4,1)S(1)}, s32[]{:S(2)}) async-start(s8[6291456]{0:T(1024)(128)(4,1)} %bitcast.110), calls=%async_computation.35 | async-start | bytes 4194304
  1329.2 86.1 %copy-start.10 = (bf16[256,2048]{1,0:T(8,128)(2,1)S(1)}, bf16[256,2048]{1,0:T(8,128)(2,1)}, u32[]{:S(2)}) copy-start(bf16[256,2048]{1,0:T(8,128)(2,1)} %param.18) | copy-start | bytes 3145732
  1329.2 88.9 %copy-start.32 = (f32[256]{0:T(256)S(1)}, f32[256]{0:T(256)}, u32[]{:S(2)}) copy-start(f32[256]{0:T(256)} %copy-done.31) | copy-start | bytes 3076
  1329.2 88.9 %copy-start.14 = (f32[256,2048]{1,0:T(8,128)S(1)}, f32[256,2048]{1,0:T(8,128)}, u32[]{:S(2)}) copy-start(f32[256,2048]{1,0:T(8,128)} %get-tuple-element.65) | copy-start | bytes 6291460
  1329.2 88.9 %copy-start.34 = (f32[256]{0:T(256)S(1)}, f32[256]{0:T(256)}, u32[]{:S(2)}) copy-start(f32[256]{0:T(256)} %copy-done.33) | copy-start | bytes 3076
  1329.2 234.1 %reduce-scatter.26.cloned.1.call-start = ((), (), s32[]{:S(2)}) async-start(), calls=%async_computation.30 | async-start | bytes 1081344 | tf_op jit(solution)/shard_map/reduce_scatter | solution.py:235
  1426.5 185.9 %reduce-scatter.20.cloned.1.call-start = ((), (), s32[]{:S(2)}) async-start(), calls=%async_computation.27 | async-start | bytes 4718592 | tf_op jit(solution)/shard_map/reduce_scatter | solution.py:240
  1433.3 348.5 %reduce-scatter.24.cloned.1.call-start = ((), (), s32[]{:S(2)}) async-start(), calls=%async_computation.29 | async-start | bytes 18874368 | tf_op jit(solution)/shard_map/reduce_scatter | solution.py:242
  1450.2 501.3 %reduce-scatter.22.cloned.1.call-start = ((), (), s32[]{:S(2)}) async-start(), calls=%async_computation.28 | async-start | bytes 18874368 | tf_op jit(solution)/shard_map/reduce_scatter | solution.py:241
  1465.5 616.5 %reduce-scatter.18.cloned.1.call-start = ((), (), s32[]{:S(2)}) async-start(), calls=%async_computation.26 | async-start | bytes 14155776 | tf_op jit(solution)/shard_map/reduce_scatter | solution.py:239
  1478.9 603.1 %copy-start.1 = (f32[256,256]{1,0:T(8,128)S(1)}, f32[256,256]{1,0:T(8,128)}, u32[]{:S(2)}) copy-start(f32[256,256]{1,0:T(8,128)} %param.23) | copy-start | bytes 786436
  1478.9 85.8 %copy-start.22 = (f32[32,128]{1,0:T(8,128)S(1)}, f32[32,128]{1,0:T(8,128)}, u32[]{:S(2)}) copy-start(f32[32,128]{1,0:T(8,128)} %copy-done.21) | copy-start | bytes 49156
  1478.9 85.8 %copy-start.24 = (f32[32,128]{1,0:T(8,128)S(1)}, f32[32,128]{1,0:T(8,128)}, u32[]{:S(2)}) copy-start(f32[32,128]{1,0:T(8,128)} %copy-done.23) | copy-start | bytes 49156
  (22 other events, 87.7 us)
Sparse Core Ops, SparseCore 0:
  11.5 54.1 all-gather.13
  75.5 52.2 all-gather.15
  129.4 64.6 all-gather.17
  214.1 47.7 all-gather.19
  356.8 85.1 reduce-scatter.9
  443.4 82.0 all-gather.23
  527.9 51.0 all-gather.21
  580.9 52.5 all-gather.29
  635.1 82.4 all-gather.27
  719.0 80.2 all-gather.31
  800.9 80.9 all-gather.25
  884.8 84.4 reduce-scatter.13
  972.4 86.3 reduce-scatter.11
  1060.2 30.5 all-gather.35
  1093.1 51.5 all-gather.33
  1146.2 64.6 all-gather.37
  1329.3 85.8 reduce-scatter.15
  1426.6 136.6 reduce-scatter.25
  1566.2 46.1 reduce-scatter.19
  1615.2 166.6 reduce-scatter.23
  1784.8 166.6 reduce-scatter.21
  1954.3 127.5 reduce-scatter.17
where the time goes:
time: 2100 us; the launch traced here: 2090 us
  waiting for transfers between devices  1650 us (79%)
  matrix products  270 us (13%)
  other arithmetic  104 us (5%)
  local copies, waits for them, and re-layouts  39.3 us (2%)
    reduce_scatter x4, waiting for transfers between devices, fold_rows(): return lax.psum_scatter(values, 'tensor', scatter_dimension=0, tiled=True)  328 us
    all_gather x4, waiting for transfers between devices, spread_rows(): return lax.all_gather(values, 'tensor', axis=0, tiled=True)  199 us
    reduce_scatter x1, waiting for transfers between devices, local(): lax.psum_scatter(grad_upw, 'dp', scatter_dimension=0, tiled=True)  170 us
    reduce_scatter x1, waiting for transfers between devices, local(): lax.psum_scatter(grad_downw, 'dp', scatter_dimension=1, tiled=True)  169 us
    all_gather x2, waiting for transfers between devices, fetch_weights(): lax.all_gather(down_part, 'dp', axis=1, tiled=True)  152 us
    all_gather x2, waiting for transfers between devices, fetch_weights(): lax.all_gather(up_part, 'dp', axis=0, tiled=True)  137 us
    reduce_scatter x1, waiting for transfers between devices, local(): lax.psum_scatter(grad_qkvw, 'dp', scatter_dimension=0, tiled=True)  130 us
    reduce_scatter x1, waiting for transfers between devices, local(): lax.psum_scatter(d_mod, ('dp', 'tensor'), scatter_dimension=1, tiled=True)  84.4 us
  transfers between devices with their start and end apart: 26, of which 23 were waited for; matrix products, arithmetic and copies ran while one was open for 16% of the time, Pallas kernels for 0%

commit v1 on v0

--- a/solution.py
+++ b/solution.py
@@ -63,7 +63,13 @@
 
 
 def fold_rows(values):
-    return lax.psum_scatter(values, "tensor", scatter_dimension=0, tiled=True)
+    low = values.astype(jnp.bfloat16)
+    return lax.psum_scatter(low, "tensor", scatter_dimension=0, tiled=True).astype(jnp.float32)
+
+
+def fold_grad(values, dim):
+    low = values.astype(jnp.bfloat16)
+    return lax.psum_scatter(low, "dp", scatter_dimension=dim, tiled=True).astype(jnp.float32)
 
 
 def local(tokens, w_qkv, w_out, w_up, w_down, w_ada, b_ada, timesteps, image_len, cotangent):
@@ -157,8 +163,6 @@
     mlp_part = jnp.dot(act_rows, full_down, preferred_element_type=jnp.float32)
     mlp_out = fold_rows(mlp_part)
     result = (mid_rows + mlp_out).astype(jnp.bfloat16)
-    held = lax.optimization_barrier((w_qkv, w_out, w_up, w_down, cotangent))
-    full_qkv, full_out, full_up, full_down = fetch_weights(held[0], held[1], held[2], held[3])
     grad_rows = cotangent.astype(jnp.float32)
     grad_full = spread_rows(cotangent)
     grad_downw = jnp.einsum("tf,td->fd", act_rows, grad_full, preferred_element_type=jnp.float32)
@@ -236,10 +240,10 @@
     grad_adaw = jnp.dot(freq.T, d_mod_cols, precision=highest)
     grad_bias = jnp.sum(d_mod_cols, axis=0)
     grad_qkvw, grad_outw, grad_upw, grad_downw = (
-        lax.psum_scatter(grad_qkvw, "dp", scatter_dimension=0, tiled=True),
-        lax.psum_scatter(grad_outw, "dp", scatter_dimension=1, tiled=True),
-        lax.psum_scatter(grad_upw, "dp", scatter_dimension=0, tiled=True),
-        lax.psum_scatter(grad_downw, "dp", scatter_dimension=1, tiled=True),
+        fold_grad(grad_qkvw, 0),
+        fold_grad(grad_outw, 1),
+        fold_grad(grad_upw, 0),
+        fold_grad(grad_downw, 1),
     )
     return (result, grad_input, grad_qkvw, grad_outw, grad_upw, grad_downw, grad_adaw, grad_bias)
 

time: 2100 us -> 1570 us (0.75)
  waiting for transfers between devices: 1650 us -> 1110 us
    reduce_scatter x8, waiting for transfers between devices: 843 us -> 407 us  [the longest x4 254 us: fold_grad(): lax.psum_scatter(low, 'dp', scatter_dimension=dim, tiled=True)]
    all_gather x2 -> x1, waiting for transfers between devices: 137 us -> 67.1 us  [fetch_weights(): lax.all_gather(up_part, 'dp', axis=0, tiled=True)]
    all_gather x2 -> x1, waiting for transfers between devices: 152 us -> 84.1 us  [fetch_weights(): lax.all_gather(down_part, 'dp', axis=1, tiled=True)]
    reduce_scatter x1, waiting for transfers between devices: 84.4 us -> 136 us  [local(): lax.psum_scatter(d_mod, ('dp', 'tensor'), scatter_dimension=1, tiled=True)]
    all_gather x2 -> x1, waiting for transfers between devices: 24.9 us -> 0.02 us  [fetch_weights(): lax.all_gather(out_part, 'dp', axis=1, tiled=True)]
    all_gather x2 -> x1, waiting for transfers between devices: 66.4 us -> 66.4 us  [fetch_weights(): lax.all_gather(qkv_part, 'dp', axis=0, tiled=True)]
  transfers between devices with their start and end apart: 26 -> 22, of which waited for: 23 -> 20; matrix products, arithmetic and copies ran while one was open for 16% -> 12% of each run, Pallas kernels for 0% -> 0%
where the time goes in v1:
time: 1570 us; the launch traced here: 1560 us
  waiting for transfers between devices  1110 us (71%)
  matrix products  271 us (17%)
  other arithmetic  117 us (7%)
  local copies, waits for them, and re-layouts  41.9 us (3%)
    reduce_scatter x4, waiting for transfers between devices, fold_grad(): lax.psum_scatter(low, 'dp', scatter_dimension=dim, tiled=True)  254 us
    all_gather x4, waiting for transfers between devices, spread_rows(): return lax.all_gather(values, 'tensor', axis=0, tiled=True)  206 us
    reduce_scatter x4, waiting for transfers between devices, fold_rows(): lax.psum_scatter(low, 'tensor', scatter_dimension=0, tiled=True)  153 us
    reduce_scatter x1, waiting for transfers between devices, local(): lax.psum_scatter(d_mod, ('dp', 'tensor'), scatter_dimension=1, tiled=True)  136 us
    all_gather x1, waiting for transfers between devices, fetch_weights(): lax.all_gather(down_part, 'dp', axis=1, tiled=True)  84.1 us
    all_gather x1, waiting for transfers between devices, fetch_weights(): lax.all_gather(up_part, 'dp', axis=0, tiled=True)  67.1 us
    all_gather x1, waiting for transfers between devices, fetch_weights(): lax.all_gather(qkv_part, 'dp', axis=0, tiled=True)  66.4 us
    ppermute x2, waiting for transfers between devices, extended_2(): lax.ppermute(lax.slice_in_dim(block, 0, width, axis=dim), axis, backward)  59.4 us
  transfers between devices with their start and end apart: 22, of which 20 were waited for; matrix products, arithmetic and copies ran while one was open for 12% of the time, Pallas kernels for 0%

profile of v1, /device:TPU:0, one launch (start us, length us, event | category | flops | bytes accessed | tf_op | source)
XLA Modules:
  0.0 1563.4 jit_solution(6132803613621453843)
XLA Ops:
  14.1 51.5 %all-gather.10.cloned.1.call-done = f32[32,8192]{1,0:T(8,128)} async-done(((f32[32,256]{1,0:T(8,128)}), f32[32,8192]{1,0:T(8,128)}) %all-gather.10.cloned.1.call-update) | async-done | bytes 1048592 | tf_op jit(solution)/shard_map/all_gather | solution.py:100
  76.2 51.6 %all-gather.12.cloned.1.call-done = bf16[1024,2048]{1,0:T(8,128)(2,1)} async-done(((bf16[256,2048]{1,0:T(8,128)(2,1)}), bf16[1024,2048]{1,0:T(8,128)(2,1)}) %all-gather.12.cloned.1.call-update) | async-done | bytes 4194320 | tf_op jit(solution)/shard_map/all_gather | solution.py:62
  127.8 66.4 %all-gather.14.cloned.1.call-done = bf16[2048,1536]{1,0:T(8,128)(2,1)} async-done(((bf16[256,1536]{1,0:T(8,128)(2,1)}), bf16[2048,1536]{1,0:T(8,128)(2,1)}) %all-gather.14.cloned.1.call-update) | async-done | bytes 6291472 | tf_op jit(solution)/shard_map/all_gather | solution.py:54
  194.2 11.2 convolution_convert_fusion.4
  218.0 59.4 %collective-permute-done.1 = bf16[1024,1024]{0,1:T(8,128)(2,1)} collective-permute-done((bf16[1024,1024]{0,1:T(8,128)(2,1)}, bf16[1024,1024]{0,1:T(8,128)(2,1)}, u32[]{:S(2)}, u32[]{:S(2)}) %collective-permute-start.1) | collective-permute-done | bytes 2097184 | tf_op jit(solution)/shard_map/ppermute | solution.py:25
  280.3 11.4 pad_maximum_fusion.1
  295.8 6.4 fusion.78
  309.7 10.7 fusion.52
  320.4 6.8 fusion.79
  334.3 9.8 fusion.53
  344.1 6.1 convolution_convert_fusion.7
  352.4 49.4 %reduce-scatter.10.cloned.1.call-done = bf16[256,2048]{1,0:T(8,128)(2,1)} async-done(((bf16[1024,2048]{1,0:T(8,128)(2,1)}), bf16[256,2048]{1,0:T(8,128)(2,1)}) %reduce-scatter.10.cloned.1.call-update) | async-done | bytes 1048592 | tf_op jit(solution)/shard_map/reduce_scatter | solution.py:67
  407.8 48.4 %all-gather.24.cloned.1.call-done = bf16[1024,2048]{1,0:T(8,128)(2,1)} async-done(((bf16[256,2048]{1,0:T(8,128)(2,1)}), bf16[1024,2048]{1,0:T(8,128)(2,1)}) %all-gather.24.cloned.1.call-update) | async-done | bytes 4194320 | tf_op jit(solution)/shard_map/all_gather | solution.py:62
  456.1 84.1 %all-gather.22.cloned.1.call-done = bf16[2048,2048]{1,0:T(8,128)(2,1)} async-done(((bf16[2048,256]{1,0:T(8,128)(2,1)}), bf16[2048,2048]{1,0:T(8,128)(2,1)}) %all-gather.22.cloned.1.call-update) | async-done | bytes 8388624 | tf_op jit(solution)/shard_map/all_gather | solution.py:57
  540.2 14.8 fusion.80
  555.0 67.1 %all-gather.20.cloned.1.call-done = bf16[2048,2048]{1,0:T(8,128)(2,1)} async-done(((bf16[256,2048]{1,0:T(8,128)(2,1)}), bf16[2048,2048]{1,0:T(8,128)(2,1)}) %all-gather.20.cloned.1.call-update) | async-done | bytes 8388624 | tf_op jit(solution)/shard_map/all_gather | solution.py:56
  622.1 53.5 %all-gather.18.cloned.1.call-done = bf16[1024,2048]{1,0:T(8,128)(2,1)} async-done(((bf16[256,2048]{1,0:T(8,128)(2,1)}), bf16[1024,2048]{1,0:T(8,128)(2,1)}) %all-gather.18.cloned.1.call-update) | async-done | bytes 4194320 | tf_op jit(solution)/shard_map/all_gather | solution.py:62
  675.6 20.2 %fusion.19 = (bf16[1024,2048]{1,0:T(8,128)(2,1)S(1)}, f32[1024,2048]{1,0:T(8,128)}) fusion(f32[1024,2048]{1,0:T(8,128)} %fusion.80, bf16[1024,2048]{1,0:T(8,128)(2,1)} %all-gather.18.cloned.1.call-done, bf16[2048,2048]{1,0:T(8,128)(2,1)} %all-gather.20.cloned.1.call-done), kind=kOutput, calls=%fused_computation.34 | convolution fusion | flops 8631877632 | bytes 33554432 | tf_op jit(solution)/shard_map/dot_general | solution.py:161
  697.8 10.6 convolution_convert_fusion.5
  708.5 15.7 %convolution_convert_fusion.6 = bf16[1024,2048]{1,0:T(8,128)(2,1)} fusion(bf16[2048,2048]{1,0:T(8,128)(2,1)} %all-gather.22.cloned.1.call-done, f32[1024,2048]{1,0:T(8,128)} %get-tuple-element.85), kind=kOutput, calls=%fused_computation.66 | convolution fusion | flops 8610906112 | bytes 20971520 | tf_op jit(solution)/shard_map/dot_general | solution.py:163
  724.3 36.9 %reduce-scatter.14.cloned.1.call-done = bf16[256,2048]{1,0:T(8,128)(2,1)} async-done(((bf16[1024,2048]{1,0:T(8,128)(2,1)}), bf16[256,2048]{1,0:T(8,128)(2,1)}) %reduce-scatter.14.cloned.1.call-update) | async-done | bytes 1048592 | tf_op jit(solution)/shard_map/reduce_scatter | solution.py:67
  763.7 53.1 %reduce-scatter.12.cloned.1.call-done = bf16[256,2048]{1,0:T(8,128)(2,1)} async-done(((bf16[1024,2048]{1,0:T(8,128)(2,1)}), bf16[256,2048]{1,0:T(8,128)(2,1)}) %reduce-scatter.12.cloned.1.call-update) | async-done | bytes 1048592 | tf_op jit(solution)/shard_map/reduce_scatter | solution.py:67
  816.8 6.4 fusion.69
  823.3 52.6 %all-gather.26.cloned.1.call-done = bf16[1024,2048]{1,0:T(8,128)(2,1)} async-done(((bf16[256,2048]{1,0:T(8,128)(2,1)}), bf16[1024,2048]{1,0:T(8,128)(2,1)}) %all-gather.26.cloned.1.call-update) | async-done | bytes 4194320 | tf_op jit(solution)/shard_map/all_gather | solution.py:62
  882.0 13.3 fusion.30
  895.3 13.7 multiply_reduce_fusion.1
  912.6 13.6 multiply_reduce_fusion
  926.2 9.3 fusion.28
  935.6 22.0 %multiply_convert_fusion.1 = bf16[4,512,2560]{2,1,0:T(8,128)(2,1)} fusion(f32[4,512,2560]{2,1,0:T(8,128)} %get-tuple-element.87, f32[4,512,2560]{2,1,0:T(8,128)} %copy-done.3, f32[4,512]{1,0:T(4,128)S(1)} %get-tuple-element.86, f32[4,512]{1,0:T(4,128)S(1)} %log_add_fusion.1), kind=kLoop, calls=%fused_computation.3 | loop fusion | flops 20971520 | bytes 52445184 | tf_op jit(solution)/shard_map/convert_element_type | solution.py:197
  957.6 8.9 multiply_bitcast_fusion
  966.5 6.1 scatter-add.14
  972.6 14.4 multiply_convert_fusion
  987.1 9.6 fusion.29
  996.7 8.2 fusion.4
  1013.4 8.4 fusion.54
  1021.8 6.1 fusion.55
  1029.1 29.0 %collective-permute-done.2 = bf16[1024,1024]{0,1:T(8,128)(2,1)} collective-permute-done((bf16[1024,1024]{0,1:T(8,128)(2,1)}, bf16[1024,1024]{0,1:T(8,128)(2,1)}, u32[]{:S(2)}, u32[]{:S(2)}) %collective-permute-start.2) | collective-permute-done | bytes 2097184 | tf_op jit(solution)/shard_map/ppermute | solution.py:22
  1065.8 11.1 convolution_convert_fusion.3
  1077.0 14.2 convolution_convert_fusion.1
  1091.2 15.9 %convolution_convert_fusion = bf16[2048,2048]{1,0:T(8,128)(2,1)} fusion(bf16[1024,2048]{1,0:T(8,128)(2,1)} %all-gather.24.cloned.1.call-done, f32[1024,2048]{1,0:T(8,128)} %get-tuple-element.85), kind=kOutput, calls=%fused_computation.44 | convolution fusion | flops 8613003264 | bytes 20971520 | tf_op jit(solution)/shard_map/tf,td->fd/dot_general | solution.py:168
  1108.3 5.9 convolution_convert_fusion.8
  1115.9 13.3 reduce-scatter.16.cloned.1.call-done
  1141.5 11.4 convolution_convert_fusion.2
  1153.0 67.9 %reduce-scatter.22.cloned.1.call-done = bf16[256,2048]{1,0:T(8,128)(2,1)} async-done(((bf16[2048,2048]{1,0:T(8,128)(2,1)}), bf16[256,2048]{1,0:T(8,128)(2,1)}) %reduce-scatter.22.cloned.1.call-update) | async-done | bytes 1048592 | tf_op jit(solution)/shard_map/reduce_scatter | solution.py:72
  1223.7 87.4 %reduce-scatter.24.cloned.1.call-done = bf16[2048,256]{1,0:T(8,128)(2,1)} async-done(((bf16[2048,2048]{1,0:T(8,128)(2,1)}), bf16[2048,256]{1,0:T(8,128)(2,1)}) %reduce-scatter.24.cloned.1.call-update) | async-done | bytes 1048592 | tf_op jit(solution)/shard_map/reduce_scatter | solution.py:72
  1313.7 34.0 %reduce-scatter.20.cloned.1.call-done = bf16[512,256]{1,0:T(8,128)(2,1)} async-done(((bf16[512,2048]{1,0:T(8,128)(2,1)}), bf16[512,256]{1,0:T(8,128)(2,1)}) %reduce-scatter.20.cloned.1.call-update) | async-done | bytes 262160 | tf_op jit(solution)/shard_map/reduce_scatter | solution.py:72
  1349.5 136.2 %reduce-scatter.26.cloned.1.call-done = f32[32,256]{1,0:T(8,128)} async-done(((f32[32,8192]{1,0:T(8,128)}), f32[32,256]{1,0:T(8,128)}) %reduce-scatter.26.cloned.1.call-update) | async-done | bytes 32784 | tf_op jit(solution)/shard_map/reduce_scatter | solution.py:239
  1489.0 64.6 %reduce-scatter.18.cloned.1.call-done = bf16[256,1536]{1,0:T(8,128)(2,1)} async-done(((bf16[2048,1536]{1,0:T(8,128)(2,1)}), bf16[256,1536]{1,0:T(8,128)(2,1)}) %reduce-scatter.18.cloned.1.call-update) | async-done | bytes 786448 | tf_op jit(solution)/shard_map/reduce_scatter | solution.py:72
  (203 shorter events, 119.3 us)
Async XLA Ops:
  7.2 58.5 %all-gather.10.cloned.1.call-start = ((), (), s32[]{:S(2)}) async-start(), calls=%async_computation.9 | async-start | bytes 1081344 | tf_op jit(solution)/shard_map/all_gather | solution.py:100
  10.2 117.6 %all-gather.12.cloned.1.call-start = ((), (), s32[]{:S(2)}) async-start(), calls=%async_computation.10 | async-start | bytes 5242880 | tf_op jit(solution)/shard_map/all_gather | solution.py:62
  14.1 56.3 %copy-start.33 = (f32[256]{0:T(256)}, f32[256]{0:T(256)S(1)}, u32[]{:S(2)}) copy-start(f32[256]{0:T(256)S(1)} %fusion.62) | copy-start | bytes 3076
  14.1 56.3 %copy-start.29 = (s32[256]{0:T(256)}, s32[256]{0:T(256)S(1)}, u32[]{:S(2)}) copy-start(s32[256]{0:T(256)S(1)} %broadcast_add_fusion.1) | copy-start | bytes 3076
  14.1 59.6 %copy-start.6 = (bf16[256,2048]{1,0:T(8,128)(2,1)S(1)}, bf16[256,2048]{1,0:T(8,128)(2,1)}, u32[]{:S(2)}) copy-start(bf16[256,2048]{1,0:T(8,128)(2,1)} %param.18) | copy-start | bytes 3145732
  75.4 118.8 %all-gather.14.cloned.1.call-start = ((), (), s32[]{:S(2)}) async-start(), calls=%async_computation.11 | async-start | bytes 7077888 | tf_op jit(solution)/shard_map/all_gather | solution.py:54
  76.1 268.0 %all-gather.16.cloned.1.call-start = ((), (), s32[]{:S(2)}) async-start(), calls=%async_computation.12 | async-start | bytes 2359296 | tf_op jit(solution)/shard_map/all_gather | solution.py:55
  214.3 63.1 %collective-permute-start.1 = (bf16[1024,1024]{0,1:T(8,128)(2,1)}, bf16[1024,1024]{0,1:T(8,128)(2,1)}, u32[]{:S(2)}, u32[]{:S(2)}) collective-permute-start(bf16[1024,1024]{0,1:T(8,128)(2,1)} %pad_maximum_fusion.6), channel_id=1, source_target_pairs={{4,0},{8,4},{12,8},{16,12},{20,16},{24,20},{28,24},{0,28},{5,1},{9... | collective-permute-start | bytes 6291464 | tf_op jit(solution)/shard_map/ppermute | solution.py:25
  214.9 65.4 %collective-permute-start = (bf16[1024,1024]{0,1:T(8,128)(2,1)}, bf16[1024,1024]{0,1:T(8,128)(2,1)}, u32[]{:S(2)}, u32[]{:S(2)}) collective-permute-start(bf16[1024,1024]{0,1:T(8,128)(2,1)} %pad_maximum_fusion.6), channel_id=1, source_target_pairs={{0,4},{4,8},{8,12},{12,16},{16,20},{20,24},{24,28},{28,0},{1,5},{5... | collective-permute-start | bytes 6291464 | tf_op jit(solution)/shard_map/ppermute | solution.py:22
  214.9 186.9 %reduce-scatter.10.cloned.1.call-start = ((), (), s32[]{:S(2)}) async-start(), calls=%async_computation.13 | async-start | bytes 5242880 | tf_op jit(solution)/shard_map/reduce_scatter | solution.py:67
  350.3 105.9 %all-gather.24.cloned.1.call-start = ((), (), s32[]{:S(2)}) async-start(), calls=%async_computation.18 | async-start | bytes 5242880 | tf_op jit(solution)/shard_map/all_gather | solution.py:62
  350.9 189.4 %all-gather.22.cloned.1.call-start = ((), (), s32[]{:S(2)}) async-start(), calls=%async_computation.16 | async-start | bytes 9437184 | tf_op jit(solution)/shard_map/all_gather | solution.py:57
  351.6 270.5 %all-gather.20.cloned.1.call-start = ((), (), s32[]{:S(2)}) async-start(), calls=%async_computation.15 | async-start | bytes 9437184 | tf_op jit(solution)/shard_map/all_gather | solution.py:56
  352.3 323.2 %all-gather.18.cloned.1.call-start = ((), (), s32[]{:S(2)}) async-start(), calls=%async_computation.14 | async-start | bytes 5242880 | tf_op jit(solution)/shard_map/all_gather | solution.py:62
  407.7 353.5 %reduce-scatter.14.cloned.1.call-start = ((), (), s32[]{:S(2)}) async-start(), calls=%async_computation.19 | async-start | bytes 5242880 | tf_op jit(solution)/shard_map/reduce_scatter | solution.py:67
  675.6 22.2 %copy-start.35 = (bf16[2048,2048]{1,0:T(8,128)(2,1)S(1)}, bf16[2048,2048]{1,0:T(8,128)(2,1)}, u32[]{:S(2)}) copy-start(bf16[2048,2048]{1,0:T(8,128)(2,1)} %all-gather.20.cloned.1.call-done) | copy-start | bytes 25165828
  708.4 108.4 %reduce-scatter.12.cloned.1.call-start = ((), (), s32[]{:S(2)}) async-start(), calls=%async_computation.17 | async-start | bytes 5242880 | tf_op jit(solution)/shard_map/reduce_scatter | solution.py:67
  724.2 37.0 %copy-start.9 = (bf16[256,2048]{1,0:T(8,128)(2,1)S(1)}, bf16[256,2048]{1,0:T(8,128)(2,1)}, u32[]{:S(2)}) copy-start(bf16[256,2048]{1,0:T(8,128)(2,1)} %reduce-scatter.10.cloned.1.call-done) | copy-start | bytes 3145732
  724.2 151.7 %all-gather.26.cloned.1.call-start = ((), (), s32[]{:S(2)}) async-start(), calls=%async_computation.20 | async-start | bytes 5242880 | tf_op jit(solution)/shard_map/all_gather | solution.py:62
  763.7 59.6 %copy-start.26 = (f32[4,512]{1,0:T(4,128)S(1)}, f32[4,512]{1,0:T(4,128)}, u32[]{:S(2)}) copy-start(f32[4,512]{1,0:T(4,128)} %copy-done.25) | copy-start | bytes 24580
  763.7 59.6 %copy-start.28 = (f32[4,512]{1,0:T(4,128)S(1)}, f32[4,512]{1,0:T(4,128)}, u32[]{:S(2)}) copy-start(f32[4,512]{1,0:T(4,128)} %copy-done.27) | copy-start | bytes 24580
  823.2 306.0 %reduce-scatter.16.cloned.1.call-start = ((), (), s32[]{:S(2)}) async-start(), calls=%async_computation.21 | async-start | bytes 5242880 | tf_op jit(solution)/shard_map/reduce_scatter | solution.py:67
  882.0 13.3 copy-start.11
  935.5 22.0 %copy-start.4 = (f32[3072,4,128]{0,2,1:T(8,128)}, f32[3072,4,128]{0,2,1:T(8,128)S(1)}, u32[]{:S(2)}) copy-start(f32[3072,4,128]{0,2,1:T(8,128)S(1)} %fusion.28) | copy-start | bytes 18874372
  935.5 37.0 %slice-start = ((s8[20971520]{0:T(1024)(128)(4,1)}), s8[4194304]{0:T(1024)(128)(4,1)S(1)}, s32[]{:S(2)}) async-start(s8[20971520]{0:T(1024)(128)(4,1)} %bitcast.94), calls=%async_computation.27 | async-start | bytes 8388608
  935.6 37.0 %slice-start.1 = ((s8[20971520]{0:T(1024)(128)(4,1)}), s8[4194304]{0:T(1024)(128)(4,1)S(1)}, s32[]{:S(2)}) async-start(s8[20971520]{0:T(1024)(128)(4,1)} %bitcast.94), calls=%async_computation.28 | async-start | bytes 8388608
  935.6 37.0 %slice-start.2 = ((s8[20971520]{0:T(1024)(128)(4,1)}), s8[4194304]{0:T(1024)(128)(4,1)S(1)}, s32[]{:S(2)}) async-start(s8[20971520]{0:T(1024)(128)(4,1)} %bitcast.94), calls=%async_computation.29 | async-start | bytes 8388608
  935.6 37.0 %slice-start.3 = ((s8[20971520]{0:T(1024)(128)(4,1)}), s8[4194304]{0:T(1024)(128)(4,1)S(1)}, s32[]{:S(2)}) async-start(s8[20971520]{0:T(1024)(128)(4,1)} %bitcast.94), calls=%async_computation.30 | async-start | bytes 8388608
  957.6 15.1 slice-start.4
  1009.8 48.2 %collective-permute-start.2 = (bf16[1024,1024]{0,1:T(8,128)(2,1)}, bf16[1024,1024]{0,1:T(8,128)(2,1)}, u32[]{:S(2)}, u32[]{:S(2)}) collective-permute-start(bf16[1024,1024]{0,1:T(8,128)(2,1)} %get-tuple-element.58), channel_id=1, source_target_pairs={{0,4},{4,8},{8,12},{12,16},{16,20},{20,24},{24,28},{28,0},{1,5},{5... | collective-permute-start | bytes 6291464 | tf_op jit(solution)/shard_map/ppermute | solution.py:22
  1009.8 11.9 slice-start.5
  1009.9 11.9 slice-start.6
  1009.9 11.9 slice-start.7
  1009.9 48.2 %collective-permute-start.3 = (bf16[1024,1024]{0,1:T(8,128)(2,1)}, bf16[1024,1024]{0,1:T(8,128)(2,1)}, u32[]{:S(2)}, u32[]{:S(2)}) collective-permute-start(bf16[1024,1024]{0,1:T(8,128)(2,1)} %get-tuple-element.59), channel_id=1, source_target_pairs={{4,0},{8,4},{12,8},{16,12},{20,16},{24,20},{28,24},{0,28},{5,1},{9... | collective-permute-start | bytes 6291464 | tf_op jit(solution)/shard_map/ppermute | solution.py:25
  1013.4 44.7 %slice-start.8 = ((s8[6291456]{0:T(1024)(128)(4,1)}), s8[4194304]{0:T(1024)(128)(4,1)S(1)}, s32[]{:S(2)}) async-start(s8[6291456]{0:T(1024)(128)(4,1)} %bitcast.99), calls=%async_computation.35 | async-start | bytes 8388608
  1021.8 36.3 %slice-start.9 = ((s8[6291456]{0:T(1024)(128)(4,1)}), s8[2097152]{0:T(1024)(128)(4,1)S(1)}, s32[]{:S(2)}) async-start(s8[6291456]{0:T(1024)(128)(4,1)} %bitcast.99), calls=%async_computation.36 | async-start | bytes 4194304
  1076.9 143.9 %reduce-scatter.22.cloned.1.call-start = ((), (), s32[]{:S(2)}) async-start(), calls=%async_computation.24 | async-start | bytes 9437184 | tf_op jit(solution)/shard_map/reduce_scatter | solution.py:72
  1091.2 219.9 %reduce-scatter.24.cloned.1.call-start = ((), (), s32[]{:S(2)}) async-start(), calls=%async_computation.25 | async-start | bytes 9437184 | tf_op jit(solution)/shard_map/reduce_scatter | solution.py:72
  1107.2 240.6 %reduce-scatter.20.cloned.1.call-start = ((), (), s32[]{:S(2)}) async-start(), calls=%async_computation.23 | async-start | bytes 2359296 | tf_op jit(solution)/shard_map/reduce_scatter | solution.py:72
  1114.2 16.5 %copy-start.7 = (bf16[256,2048]{1,0:T(8,128)(2,1)S(1)}, bf16[256,2048]{1,0:T(8,128)(2,1)}, u32[]{:S(2)}) copy-start(bf16[256,2048]{1,0:T(8,128)(2,1)} %param.18) | copy-start | bytes 3145732
  1114.3 371.5 %reduce-scatter.26.cloned.1.call-start = ((), (), s32[]{:S(2)}) async-start(), calls=%async_computation.26 | async-start | bytes 1081344 | tf_op jit(solution)/shard_map/reduce_scatter | solution.py:239
  1115.9 17.2 %copy-start.32 = (f32[256]{0:T(256)S(1)}, f32[256]{0:T(256)}, u32[]{:S(2)}) copy-start(f32[256]{0:T(256)} %copy-done.31) | copy-start | bytes 3076
  1115.9 17.2 %copy-start.15 = (f32[256,2048]{1,0:T(8,128)S(1)}, f32[256,2048]{1,0:T(8,128)}, u32[]{:S(2)}) copy-start(f32[256,2048]{1,0:T(8,128)} %get-tuple-element.57) | copy-start | bytes 6291460
  1115.9 17.2 %copy-start.34 = (f32[256]{0:T(256)S(1)}, f32[256]{0:T(256)}, u32[]{:S(2)}) copy-start(f32[256]{0:T(256)} %copy-done.33) | copy-start | bytes 3076
  1141.5 412.1 %reduce-scatter.18.cloned.1.call-start = ((), (), s32[]{:S(2)}) async-start(), calls=%async_computation.22 | async-start | bytes 7077888 | tf_op jit(solution)/shard_map/reduce_scatter | solution.py:72
  1153.0 334.1 %copy-start.22 = (f32[32,128]{1,0:T(8,128)S(1)}, f32[32,128]{1,0:T(8,128)}, u32[]{:S(2)}) copy-start(f32[32,128]{1,0:T(8,128)} %copy-done.21) | copy-start | bytes 49156
  1153.0 334.1 %copy-start.24 = (f32[32,128]{1,0:T(8,128)S(1)}, f32[32,128]{1,0:T(8,128)}, u32[]{:S(2)}) copy-start(f32[32,128]{1,0:T(8,128)} %copy-done.23) | copy-start | bytes 49156
  1153.0 403.1 %copy-start.1 = (f32[256,256]{1,0:T(8,128)S(1)}, f32[256,256]{1,0:T(8,128)}, u32[]{:S(2)}) copy-start(f32[256,256]{1,0:T(8,128)} %param.23) | copy-start | bytes 786436
  (25 other events, 107.8 us)
Sparse Core Ops, SparseCore 0:
  11.5 54.1 all-gather.9
  75.5 52.2 all-gather.11
  129.5 64.6 all-gather.13
  215.1 47.7 all-gather.15
  350.4 51.3 reduce-scatter.9
  403.5 52.5 all-gather.23
  457.7 82.4 all-gather.21
  541.8 80.2 all-gather.19
  624.5 51.0 all-gather.17
  708.5 52.5 reduce-scatter.13
  764.2 52.5 reduce-scatter.11
  823.3 52.5 all-gather.25
  1077.1 52.0 reduce-scatter.15
  1131.3 89.5 reduce-scatter.21
  1223.0 87.9 reduce-scatter.23
  1313.2 34.5 reduce-scatter.19
  1350.4 135.2 reduce-scatter.25
  1487.9 65.6 reduce-scatter.17
